TPU v7x, 32 devices: a whole 2x2x4 slice. The times are simulated.
32 devices in a mesh: parts: 2 (over y), seq: 4 (over z), sub: 4 (over x, core).
Axes of the slice: x: 2, y: 2, z: 4, core: 2. Of those that a mesh axis runs over, the one named last changes fastest.
Arguments:
- q_space: bfloat16 [16, 512, 2048], P(('parts', 'seq'), None, 'sub'), parts along dimension 0, may hold values from -6 to 6
- k_space: bfloat16 [16, 512, 2048], P(('parts', 'seq'), None, 'sub'), parts along dimension 0, may hold values from -6 to 6
- v_space: bfloat16 [16, 512, 2048], P(('parts', 'seq'), None, 'sub'), parts along dimension 0, may hold values from -6 to 6
- q_time: bfloat16 [16, 4, 128, 2048], P('parts', None, 'seq', 'sub'), parts along dimension 0, may hold values from -6 to 6
- k_time: bfloat16 [16, 4, 128, 2048], P('parts', None, 'seq', 'sub'), parts along dimension 0, may hold values from -6 to 6
- out_weight: bfloat16 [2048, 3072], P('sub', 'seq'), may hold values from -0.125 to 0.125
- cotangent: bfloat16 [16, 512, 3072], P(('parts', 'seq'), 'sub'), parts along dimension 0, may hold values from -6 to 6
Outputs:
- dq_space: bfloat16 [16, 512, 2048], P(('parts', 'seq'), None, 'sub'), parts along dimension 0
- dk_space: bfloat16 [16, 512, 2048], P(('parts', 'seq'), None, 'sub'), parts along dimension 0
- dv_space: bfloat16 [16, 512, 2048], P(('parts', 'seq'), None, 'sub'), parts along dimension 0
- d_weight: float32 [4096, 3072], P(('parts', 'sub'), 'seq'), parts along dimension 0
There are 2 independent parts, one for each index of `parts`. A program takes and returns all parts, laid end to end along the dimension named above; an argument that names none is the same for every part. Nothing has to cross between parts.
All inputs are finite; a program needn't handle non-finite values.
Results may differ from a plain program's by a relative error of at most 0.01.
Values may be sent and summed in bfloat16 or wider, within the bound.
No kernel may reach another device: no remote copies, remote signals or barrier semaphores. Data moves between devices by JAX's collectives and lax.ppermute only.
A program may use at most 128 MiB of HBM per device.

v0:
```python
import math
import jax
import jax.numpy as jnp
from jax import lax
from jax.sharding import PartitionSpec as P

HD = 128


def normalize(scores):
    row_top = jnp.max(scores, axis=-1, keepdims=True)
    raised = jnp.exp(scores - row_top)
    return raised / jnp.sum(raised, axis=-1, keepdims=True)


def space_chances(query, keys):
    scores = jnp.einsum("fqhd,fkhd->fhqk", query, keys, preferred_element_type=jnp.float32) * (
        1.0 / math.sqrt(HD)
    )
    return normalize(scores)


def on_device(q_space, k_space, v_space, q_time, k_time, out_weight, cotangent):
    frame_count, patches, columns = q_space.shape
    head_count = columns // HD
    band_count = lax.axis_size("sub")
    seq_count = lax.axis_size("seq")
    all_frames = frame_count * seq_count
    band_len = patches // band_count
    time_len = band_len // seq_count
    split_shape = (frame_count, patches, head_count, HD)
    space_query = q_space.reshape(split_shape)
    space_keys = k_space.reshape(split_shape)
    space_values = v_space.reshape(split_shape)
    chances = space_chances(space_query, space_keys)
    space_out = jnp.einsum(
        "fhqk,fkhd->fqhd",
        chances.astype(jnp.bfloat16),
        space_values,
        preferred_element_type=jnp.float32,
    ).astype(jnp.bfloat16)
    moved = lax.all_to_all(
        space_out.reshape(frame_count, band_count, band_len, columns),
        "seq",
        split_axis=2,
        concat_axis=0,
        tiled=True,
    )
    time_shape = (all_frames, band_count, time_len, head_count, HD)
    time_query = q_time.reshape(time_shape)
    time_keys = k_time.reshape(time_shape)
    time_values = moved.reshape(time_shape)
    time_scores = jnp.einsum(
        "fbphd,gbphd->bphfg", time_query, time_keys, preferred_element_type=jnp.float32
    ) * (1.0 / math.sqrt(HD))
    time_chances = normalize(time_scores).astype(jnp.bfloat16)
    time_out = jnp.einsum(
        "bphfg,gbphd->fbphd", time_chances, time_values, preferred_element_type=jnp.float32
    ).astype(jnp.bfloat16)
    time_out = time_out.reshape(all_frames, band_count, time_len, columns)
    weight_rows = lax.all_gather(out_weight, "seq", axis=1, tiled=True)
    returned = lax.all_to_all(time_out, "seq", split_axis=0, concat_axis=2, tiled=True)
    frame_out = returned.reshape(frame_count, patches, columns)
    segment = lax.all_gather(cotangent, "sub", axis=1, tiled=True)
    weight_sum = jnp.einsum("fnh,fnd->hd", frame_out, segment, preferred_element_type=jnp.float32)
    update = jnp.einsum("fnd,hd->fnh", segment, weight_rows, preferred_element_type=jnp.float32)
    out_grad = update
    weight_sum, out_grad = (weight_sum, out_grad)
    rounded = out_grad.astype(jnp.bfloat16).reshape(frame_count, band_count, band_len, columns)
    time_grad = lax.all_to_all(rounded, "seq", split_axis=2, concat_axis=0, tiled=True)
    d_weight = lax.psum_scatter(
        weight_sum.astype(jnp.bfloat16), "seq", scatter_dimension=1, tiled=True
    ).astype(jnp.float32)
    value_time = jnp.einsum(
        "bphfg,fbphd->gbphd",
        time_chances,
        time_grad.reshape(time_shape),
        preferred_element_type=jnp.float32,
    ).astype(jnp.bfloat16)
    space_grad = lax.all_to_all(
        value_time.reshape(all_frames, band_count, time_len, columns),
        "seq",
        split_axis=0,
        concat_axis=2,
        tiled=True,
    )
    space_grad = space_grad.reshape(split_shape)
    recomputed = space_chances(space_query, space_keys)
    value_grad = jnp.einsum(
        "fhqk,fqhd->fkhd",
        recomputed.astype(jnp.bfloat16),
        space_grad,
        preferred_element_type=jnp.float32,
    ).astype(jnp.bfloat16)
    chance_grad = jnp.einsum(
        "fqhd,fkhd->fhqk", space_grad, space_values, preferred_element_type=jnp.float32
    )
    centre_term = jnp.sum(recomputed * chance_grad, axis=-1, keepdims=True)
    score_grad = (recomputed * (chance_grad - centre_term) * (1.0 / math.sqrt(HD))).astype(
        jnp.bfloat16
    )
    query_grad = jnp.einsum(
        "fhqk,fkhd->fqhd", score_grad, space_keys, preferred_element_type=jnp.float32
    ).astype(jnp.bfloat16)
    keys_grad = jnp.einsum(
        "fhqk,fqhd->fkhd", score_grad, space_query, preferred_element_type=jnp.float32
    ).astype(jnp.bfloat16)
    flat_shape = (frame_count, patches, columns)
    return (
        query_grad.reshape(flat_shape),
        keys_grad.reshape(flat_shape),
        value_grad.reshape(flat_shape),
        d_weight,
    )


def solution(mesh):
    in_specs = (
        P(("parts", "seq"), None, "sub"),
        P(("parts", "seq"), None, "sub"),
        P(("parts", "seq"), None, "sub"),
        P("parts", None, "seq", "sub"),
        P("parts", None, "seq", "sub"),
        P("sub", "seq"),
        P(("parts", "seq"), "sub", None),
    )
    out_specs = (
        P(("parts", "seq"), None, "sub"),
        P(("parts", "seq"), None, "sub"),
        P(("parts", "seq"), None, "sub"),
        P(("parts", "sub"), "seq"),
    )
    return jax.shard_map(
        on_device, mesh=mesh, in_specs=in_specs, out_specs=out_specs, check_vma=False
    )
```

profile of v0, /device:TPU:0, one launch (start us, length us, event | category | flops | bytes accessed | tf_op | source)
XLA Modules:
  0.0 300.6 jit_solution(187689830887894949)
XLA Ops:
  7.2 0.0 copy-start
  7.2 0.0 all-gather.3.cloned.1.call-start
  7.2 0.7 all-gather.3.cloned.1.call-update
  7.9 0.0 all-gather.5.cloned.1.call-start
  8.0 0.7 all-gather.5.cloned.1.call-update
  8.7 1.5 copy.121
  10.2 0.0 copy-start.1
  10.2 1.9 copy.120
  12.1 0.0 copy-start.3
  12.1 5.1 %fusion.79 = (f32[2,4,512]{2,1,0:T(4,128)S(1)}, f32[2,4,512,512]{2,3,1,0:T(8,128)}) fusion(bf16[2,512,4,128]{1,3,2,0:T(8,128)(2,1)S(1)} %bitcast.79, bf16[2,512,4,128]{1,3,2,0:T(8,128)(2,1)S(1)} %bitcast.81), kind=kOutput, calls=%fused_computation.55 | convolution fusion | flops 543162880 | bytes 10502144 | tf_op jit(solution)/shard_map/sub | solution.py:12
  17.1 0.0 copy-done.1
  17.1 0.0 copy-done
  17.1 5.8 %fusion.40 = bf16[2,512,4,128]{3,1,2,0:T(8,128)(2,1)S(1)} fusion(f32[2,4,512,512]{2,3,1,0:T(8,128)} %get-tuple-element.23, f32[2,4,512]{2,1,0:T(4,128)S(1)} %get-tuple-element.22, bf16[2,512,512]{2,1,0:T(8,128)(2,1)S(1)} %copy-done), kind=kOutput, calls=%fused_computation.33 | convolution fusion | flops 541589504 | bytes 10502144 | tf_op jit(solution)/shard_map/fhqk,fkhd->fqhd/dot_general | solution.py:36
  22.9 0.0 copy-done.3
  22.9 0.8 copy.103
  23.7 0.4 reshape.77
  24.2 1.8 copy.104
  26.0 6.5 %all-to-all-start.2 = ((bf16[2,4,128,512]{3,1,0,2:T(4,128)(2,1)}), bf16[2,4,128,512]{3,1,0,2:T(4,128)(2,1)S(1)}, u32[]{:S(2)}, u32[]{:S(2)}) async-start(bf16[2,4,128,512]{3,1,0,2:T(4,128)(2,1)} %copy.104), calls=%async_computation.2 | async-start | bytes 2097152 | tf_op jit(solution)/shard_map/all_to_all | solution.py:42
  32.5 0.0 reduce-scatter.2.cloned.1.call-start
  32.5 1.4 reshape.69
  33.8 2.1 reshape.70
  36.0 4.8 %fusion.74 = (f32[4,32,4,8]{3,2,1,0:T(4,128)S(1)}, f32[4,32,4,8,8]{3,4,2,1,0:T(8,128)}) fusion(bf16[8,4,32,4,128]{4,3,2,1,0:T(4,128)(2,1)} %reshape.70, bf16[8,4,32,4,128]{4,3,2,1,0:T(4,128)(2,1)S(1)} %reshape.69), kind=kOutput, calls=%fused_computation.54 | convolution fusion | flops 8486919 | bytes 2244608 | tf_op jit(solution)/shard_map/sub | solution.py:12
  40.7 17.3 %all-to-all-done.2 = bf16[2,4,128,512]{3,1,0,2:T(4,128)(2,1)S(1)} async-done(((bf16[2,4,128,512]{3,1,0,2:T(4,128)(2,1)}), bf16[2,4,128,512]{3,1,0,2:T(4,128)(2,1)S(1)}, u32[]{:S(2)}, u32[]{:S(2)}) %all-to-all-start.2) | async-done | bytes 1048608 | tf_op jit(solution)/shard_map/all_to_all | solution.py:42
  58.0 0.3 copy.157
  58.3 0.3 reshape.78
  58.6 2.6 fusion.39
  61.2 0.6 copy.108
  61.8 0.4 reshape.79
  62.2 52.4 %all_to_all.60 = bf16[8,4,32,512]{3,2,1,0:T(8,128)(2,1)S(1)} all-to-all(bf16[8,4,32,512]{3,2,1,0:T(8,128)(2,1)S(1)} %reshape.79), channel_id=1, replica_groups=mesh['parts'=2,'seq'=4,'sub'=4] {'seq'}, dimensions={0} | all-to-all | bytes 2097152 | tf_op jit(solution)/shard_map/all_to_all | solution.py:62
  114.6 0.1 copy.109
  114.7 0.0 all-gather.3.cloned.1.call-done
  114.8 7.6 %bitcast_convert_fusion = bf16[512,3072]{1,0:T(8,128)(2,1)} fusion(bf16[2,512,512]{2,1,0:T(8,128)(2,1)S(1)} %bitcast.83, bf16[2,512,3072]{2,1,0:T(8,128)(2,1)} %all-gather.3.cloned.1.call-done), kind=kOutput, calls=%fused_computation.9 | convolution fusion | flops 3222798336 | bytes 10485760 | tf_op jit(solution)/shard_map/fnh,fnd->hd/dot_general | solution.py:65
  122.4 0.0 reduce-scatter.2.cloned.1.call-update
  122.4 18.3 %all-gather.5.cloned.1.call-done = bf16[512,3072]{1,0:T(8,128)(2,1)} async-done(((bf16[512,768]{1,0:T(8,128)(2,1)}), bf16[512,3072]{1,0:T(8,128)(2,1)}) %all-gather.5.cloned.1.call-update) | async-done | bytes 3145744 | tf_op jit(solution)/shard_map/all_gather | solution.py:61
  140.8 7.1 %fusion.35 = bf16[2,512,512]{2,1,0:T(8,128)(2,1)S(1)} fusion(bf16[2,512,3072]{2,1,0:T(8,128)(2,1)} %all-gather.3.cloned.1.call-done, bf16[512,3072]{1,0:T(8,128)(2,1)} %all-gather.5.cloned.1.call-done), kind=kOutput, calls=%fused_computation.30 | convolution fusion | flops 3221749760 | bytes 10485760 | tf_op jit(solution)/shard_map/fnd,hd->fnh/dot_general | solution.py:66
  147.9 0.8 copy.85
  148.7 57.4 %all_to_all.61 = bf16[2,4,128,512]{3,1,0,2:T(4,128)(2,1)S(1)} all-to-all(bf16[2,4,128,512]{3,1,0,2:T(4,128)(2,1)S(1)} %copy.85), channel_id=1, replica_groups=mesh['parts'=2,'seq'=4,'sub'=4] {'seq'}, dimensions={2} | all-to-all | bytes 2097152 | tf_op jit(solution)/shard_map/all_to_all | solution.py:70
  206.2 0.3 copy.86
  206.5 0.1 copy.87
  206.6 0.3 reshape.68
  206.9 2.6 fusion.38
  209.4 0.6 copy.91
  210.0 0.4 reshape.71
  210.5 36.4 %all_to_all.62 = bf16[8,4,32,512]{3,2,1,0:T(8,128)(2,1)S(1)} all-to-all(bf16[8,4,32,512]{3,2,1,0:T(8,128)(2,1)S(1)} %reshape.71), channel_id=1, replica_groups=mesh['parts'=2,'seq'=4,'sub'=4] {'seq'}, dimensions={0} | all-to-all | bytes 2097152 | tf_op jit(solution)/shard_map/all_to_all | solution.py:80
  246.8 0.1 copy.158
  246.9 0.3 reshape.72
  247.2 0.7 copy.99
  247.9 5.9 %fusion.23 = bf16[2,4,128,512]{3,2,1,0:T(8,128)(2,1)} fusion(bf16[2,512,4,128]{1,3,2,0:T(8,128)(2,1)S(1)} %copy.99, f32[2,4,512,512]{2,3,1,0:T(8,128)} %get-tuple-element.23, f32[2,4,512]{2,1,0:T(4,128)S(1)} %get-tuple-element.22), kind=kOutput, calls=%fused_computation.24 | convolution fusion | flops 541589504 | bytes 10502144 | tf_op jit(solution)/shard_map/fhqk,fqhd->fkhd/dot_general | solution.py:89
  253.7 0.0 copy-start.4
  253.8 2.4 copy.113
  256.1 4.4 %fusion.44 = f32[2,4,512,512]{2,3,1,0:T(8,128)} fusion(bf16[2,512,4,128]{1,3,2,0:T(8,128)(2,1)S(1)} %copy.99, bf16[2,512,512]{2,1,0:T(8,128)(2,1)S(1)} %copy-done), kind=kOutput, calls=%fused_computation.35 | convolution fusion | flops 536870912 | bytes 10485760 | tf_op jit(solution)/shard_map/fqhd,fkhd->fhqk/dot_general | solution.py:95
  260.6 0.0 copy-done.4
  260.6 0.0 copy-start.2
  260.6 15.2 %fusion.29 = bf16[2,4,512,128]{2,3,1,0:T(8,128)(2,1)} fusion(bf16[2,512,4,128]{1,3,2,0:T(8,128)(2,1)S(1)} %bitcast.82, f32[2,4,512,512]{2,3,1,0:T(8,128)} %fusion.44, f32[2,4,512,512]{2,3,1,0:T(8,128)} %get-tuple-element.23, f32[2,4,512]{2,1,0:T(4,128)S(1)} %get-tuple-element.22), kind=kOutput, calls=%fused_computation.26 | convolution fusion | flops 552079872 | bytes 18890752 | tf_op jit(solution)/shard_map/fhqk,fkhd->fqhd/dot_general | solution.py:102
  275.8 2.3 copy.111
  278.1 0.0 copy-done.2
  278.1 12.3 %fusion.32 = bf16[2,4,512,128]{2,3,1,0:T(8,128)(2,1)S(1)} fusion(bf16[2,512,4,128]{1,3,2,0:T(8,128)(2,1)S(1)} %bitcast.80, f32[2,4,512,512]{2,3,1,0:T(8,128)} %fusion.44, f32[2,4,512,512]{2,3,1,0:T(8,128)} %get-tuple-element.23, f32[2,4,512]{2,1,0:T(4,128)S(1)} %get-tuple-element.22), kind=kOutput, calls=%fused_computation.27 | convolution fusion | flops 552079872 | bytes 18890752 | tf_op jit(solution)/shard_map/fhqk,fqhd->fkhd/dot_general | solution.py:105
  290.3 1.3 copy.112
  291.7 0.0 reduce-scatter.2.cloned.1.call-done
  291.7 2.4 convert_element_type.72
Async XLA Ops:
  7.2 10.0 %copy-start = (bf16[2,512,512]{2,1,0:T(8,128)(2,1)S(1)}, bf16[2,512,512]{2,1,0:T(8,128)(2,1)}, u32[]{:S(2)}) copy-start(bf16[2,512,512]{2,1,0:T(8,128)(2,1)} %param.9) | copy-start | bytes 3145732
  7.2 107.6 %all-gather.3.cloned.1.call-start = ((), (), s32[]{:S(2)}) async-start(), calls=%async_computation.5 | async-start | bytes 7864320 | tf_op jit(solution)/shard_map/all_gather | solution.py:64
  7.9 132.9 %all-gather.5.cloned.1.call-start = ((), (), s32[]{:S(2)}) async-start(), calls=%async_computation.6 | async-start | bytes 3932160 | tf_op jit(solution)/shard_map/all_gather | solution.py:61
  10.2 7.0 %copy-start.1 = (bf16[2,512,512]{1,2,0:T(8,128)(2,1)}, bf16[2,512,512]{1,2,0:T(8,128)(2,1)S(1)}, u32[]{:S(2)}) copy-start(bf16[2,512,512]{1,2,0:T(8,128)(2,1)S(1)} %copy.121) | copy-start | bytes 3145732
  12.1 10.9 %copy-start.3 = (bf16[2,512,512]{1,2,0:T(8,128)(2,1)}, bf16[2,512,512]{1,2,0:T(8,128)(2,1)S(1)}, u32[]{:S(2)}) copy-start(bf16[2,512,512]{1,2,0:T(8,128)(2,1)S(1)} %copy.120) | copy-start | bytes 3145732
  26.0 32.0 %all-to-all-start.2 = ((bf16[2,4,128,512]{3,1,0,2:T(4,128)(2,1)}), bf16[2,4,128,512]{3,1,0,2:T(4,128)(2,1)S(1)}, u32[]{:S(2)}, u32[]{:S(2)}) async-start(bf16[2,4,128,512]{3,1,0,2:T(4,128)(2,1)} %copy.104), calls=%async_computation.2 | async-start | bytes 2097152 | tf_op jit(solution)/shard_map/all_to_all | solution.py:42
  32.5 259.2 %reduce-scatter.2.cloned.1.call-start = ((), (), s32[]{:S(2)}) async-start(), calls=%async_computation.7 | async-start | bytes 3932160 | tf_op jit(solution)/shard_map/reduce_scatter | solution.py:71
  253.7 6.8 %copy-start.4 = (bf16[2,512,512]{1,2,0:T(8,128)(2,1)S(1)}, bf16[2,512,512]{1,2,0:T(8,128)(2,1)}, u32[]{:S(2)}) copy-start(bf16[2,512,512]{1,2,0:T(8,128)(2,1)} %copy-done.3) | copy-start | bytes 3145732
  260.6 17.5 %copy-start.2 = (bf16[2,512,512]{1,2,0:T(8,128)(2,1)S(1)}, bf16[2,512,512]{1,2,0:T(8,128)(2,1)}, u32[]{:S(2)}) copy-start(bf16[2,512,512]{1,2,0:T(8,128)(2,1)} %copy-done.1) | copy-start | bytes 3145732
Sparse Core Ops, SparseCore 0:
  9.6 49.0 all-gather.2
  60.3 80.4 all-gather.4
  143.1 83.3 reduce-scatter.1
where the time goes:
time: 301 us
  blocking collectives  146 us (49%)
  matrix products  73.3 us (24%)
  waiting for transfers between devices  37 us (12%)
  local copies, waits for them, and re-layouts  21.2 us (7%)
  between operations  14 us (5%)
  starting transfers between devices  6.55 us (2%)
    all_to_all x1, blocking collectives, on_device(): lax.all_to_all(rounded, 'seq', split_axis=2, concat_axis=0, tiled=True)  57.4 us
    all_to_all x1, blocking collectives, on_device(): lax.all_to_all(time_out, 'seq', split_axis=0, concat_axis=2, tiled=True)  52.4 us
    all_to_all x1, blocking collectives, on_device(): lax.all_to_all(value_time.reshape(all_frames, band_count, time_len, colum...  36.4 us
    all_gather x1, waiting for transfers between devices, on_device(): weight_rows = lax.all_gather(out_weight, 'seq', axis=1, tiled=True)  18.3 us
    all_to_all x1, waiting for transfers between devices, on_device(): lax.all_to_all(space_out.reshape(frame_count, band_count, band_len, colum...  17.3 us
    dot_general x1, matrix products, on_device(): jnp.einsum('fhqk,fkhd->fqhd', score_grad, space_keys, preferred_element_t...  15.2 us
    dot_general x1, matrix products, on_device(): jnp.einsum('fhqk,fqhd->fkhd', score_grad, space_query, preferred_element_...  12.3 us
    sub x2, matrix products, normalize(): raised = jnp.exp(scores - row_top)  9.81 us
  transfers between devices with their start and end apart: 4, of which 2 were waited for; matrix products, arithmetic and copies ran while one was open for 31% of the time, Pallas kernels for 0%

commit v1 on v0

--- a/solution.py
+++ b/solution.py
@@ -58,7 +58,15 @@
         "bphfg,gbphd->fbphd", time_chances, time_values, preferred_element_type=jnp.float32
     ).astype(jnp.bfloat16)
     time_out = time_out.reshape(all_frames, band_count, time_len, columns)
-    weight_rows = lax.all_gather(out_weight, "seq", axis=1, tiled=True)
+    ways, here = (lax.axis_size("seq"), lax.axis_index("seq"))
+    grown, reach = (out_weight, 1)
+    while reach < ways:
+        theirs = lax.ppermute(grown, "seq", [(d, d ^ reach) for d in range(ways)])
+        mine_first = jnp.concatenate([grown, theirs], axis=1)
+        theirs_first = jnp.concatenate([theirs, grown], axis=1)
+        grown = jnp.where(here & reach == 0, mine_first, theirs_first)
+        reach = 2 * reach
+    weight_rows = grown
     returned = lax.all_to_all(time_out, "seq", split_axis=0, concat_axis=2, tiled=True)
     frame_out = returned.reshape(frame_count, patches, columns)
     segment = lax.all_gather(cotangent, "sub", axis=1, tiled=True)

time: 301 us -> 318 us (1.056)
  waiting for transfers between devices: 37 us -> 135 us
  blocking collectives: 146 us -> 51.1 us
  starting transfers between devices: 6.55 us -> 14.9 us
    ppermute x0 -> x2, waiting for transfers between devices: none -> 66.3 us  [on_device(): theirs = lax.ppermute(grown, 'seq', [(d, d ^ reach) for d in range(ways)])]
    all_to_all x0 -> x1, waiting for transfers between devices: none -> 52.7 us  [on_device(): lax.all_to_all(time_out, 'seq', split_axis=0, concat_axis=2, tiled=True)]
    all_to_all x1 -> x0, blocking collectives: 52.4 us -> none  [on_device(): lax.all_to_all(time_out, 'seq', split_axis=0, concat_axis=2, tiled=True)]
    all_to_all x1, blocking collectives: 57.4 us -> 24.1 us  [on_device(): lax.all_to_all(rounded, 'seq', split_axis=2, concat_axis=0, tiled=True)]
    all_gather x1 -> x0, waiting for transfers between devices: 18.3 us -> none  [on_device(): weight_rows = lax.all_gather(out_weight, 'seq', axis=1, tiled=True)]
    all_to_all x1, blocking collectives: 36.4 us -> 27 us  [on_device(): lax.all_to_all(value_time.reshape(all_frames, band_count, time_len, colum...]
    ppermute x0 -> x2, starting transfers between devices: none -> 4.47 us  [on_device(): theirs = lax.ppermute(grown, 'seq', [(d, d ^ reach) for d in range(ways)])]
    all_to_all x0 -> x1, starting transfers between devices: none -> 3.52 us  [on_device(): lax.all_to_all(time_out, 'seq', split_axis=0, concat_axis=2, tiled=True)]
  transfers between devices with their start and end apart: 4 -> 6, of which waited for: 2 -> 4; matrix products, arithmetic and copies ran while one was open for 31% -> 31% of each run, Pallas kernels for 0% -> 0%
where the time goes in v1:
time: 318 us; the launch traced here: 317 us
  waiting for transfers between devices  135 us (42%)
  matrix products  74.1 us (23%)
  blocking collectives  51.1 us (16%)
  local copies, waits for them, and re-layouts  21.9 us (7%)
  starting transfers between devices  14.9 us (5%)
  between operations  14.3 us (4%)
  other arithmetic  5.42 us (2%)
    ppermute x2, waiting for transfers between devices, on_device(): theirs = lax.ppermute(grown, 'seq', [(d, d ^ reach) for d in range(ways)])  66.3 us
    all_to_all x1, waiting for transfers between devices, on_device(): lax.all_to_all(time_out, 'seq', split_axis=0, concat_axis=2, tiled=True)  52.7 us
    all_to_all x1, blocking collectives, on_device(): lax.all_to_all(value_time.reshape(all_frames, band_count, time_len, colum...  27 us
    all_to_all x1, blocking collectives, on_device(): lax.all_to_all(rounded, 'seq', split_axis=2, concat_axis=0, tiled=True)  24.1 us
    all_to_all x1, waiting for transfers between devices, on_device(): lax.all_to_all(space_out.reshape(frame_count, band_count, band_len, colum...  15.5 us
    dot_general x1, matrix products, on_device(): jnp.einsum('fhqk,fkhd->fqhd', score_grad, space_keys, preferred_element_t...  15.2 us
    dot_general x1, matrix products, on_device(): jnp.einsum('fhqk,fqhd->fkhd', score_grad, space_query, preferred_element_...  12.3 us
    sub x2, matrix products, normalize(): raised = jnp.exp(scores - row_top)  9.8 us
  transfers between devices with their start and end apart: 6, of which 4 were waited for; matrix products, arithmetic and copies ran while one was open for 31% of the time, Pallas kernels for 0%

profile of v1, /device:TPU:0, one launch (start us, length us, event | category | flops | bytes accessed | tf_op | source)
XLA Modules:
  0.0 317.0 jit_solution(4404124092463032195)
XLA Ops:
  7.2 0.0 copy-start
  7.2 0.0 all-gather.2.cloned.1.call-start
  7.2 0.7 all-gather.2.cloned.1.call-update
  7.9 1.5 copy.121
  9.4 0.0 copy-start.1
  9.4 1.9 copy.120
  11.3 0.0 copy-start.3
  11.3 5.1 %fusion.87 = (f32[2,4,512]{2,1,0:T(4,128)S(1)}, f32[2,4,512,512]{2,3,1,0:T(8,128)}) fusion(bf16[2,512,4,128]{1,3,2,0:T(8,128)(2,1)S(1)} %bitcast.81, bf16[2,512,4,128]{1,3,2,0:T(8,128)(2,1)S(1)} %bitcast.83), kind=kOutput, calls=%fused_computation.64 | convolution fusion | flops 543162880 | bytes 10502144 | tf_op jit(solution)/shard_map/sub | solution.py:12
  16.4 0.0 copy-done.1
  16.4 0.0 copy-done
  16.4 5.5 %fusion.47 = bf16[2,512,4,128]{3,1,2,0:T(8,128)(2,1)S(1)} fusion(f32[2,4,512,512]{2,3,1,0:T(8,128)} %get-tuple-element.23, f32[2,4,512]{2,1,0:T(4,128)S(1)} %get-tuple-element.22, bf16[2,512,512]{2,1,0:T(8,128)(2,1)S(1)} %copy-done), kind=kOutput, calls=%fused_computation.41 | convolution fusion | flops 541589504 | bytes 10502144 | tf_op jit(solution)/shard_map/fhqk,fkhd->fqhd/dot_general | solution.py:36
  21.9 0.0 copy-done.3
  21.9 0.8 copy.103
  22.7 0.4 reshape.77
  23.1 1.8 copy.104
  24.9 6.7 %all-to-all-start.2 = ((bf16[2,4,128,512]{3,1,0,2:T(4,128)(2,1)}), bf16[2,4,128,512]{3,1,0,2:T(4,128)(2,1)S(1)}, u32[]{:S(2)}, u32[]{:S(2)}) async-start(bf16[2,4,128,512]{3,1,0,2:T(4,128)(2,1)} %copy.104), calls=%async_computation.2 | async-start | bytes 2097152 | tf_op jit(solution)/shard_map/all_to_all | solution.py:42
  31.6 2.0 collective-permute-start
  33.6 1.3 reshape.69
  35.0 2.1 reshape.70
  37.1 4.8 %fusion.82 = (f32[4,32,4,8]{3,2,1,0:T(4,128)S(1)}, f32[4,32,4,8,8]{3,4,2,1,0:T(8,128)}) fusion(bf16[8,4,32,4,128]{4,3,2,1,0:T(4,128)(2,1)} %reshape.70, bf16[8,4,32,4,128]{4,3,2,1,0:T(4,128)(2,1)S(1)} %reshape.69), kind=kOutput, calls=%fused_computation.63 | convolution fusion | flops 8486919 | bytes 2244608 | tf_op jit(solution)/shard_map/sub | solution.py:12
  41.8 15.5 %all-to-all-done.2 = bf16[2,4,128,512]{3,1,0,2:T(4,128)(2,1)S(1)} async-done(((bf16[2,4,128,512]{3,1,0,2:T(4,128)(2,1)}), bf16[2,4,128,512]{3,1,0,2:T(4,128)(2,1)S(1)}, u32[]{:S(2)}, u32[]{:S(2)}) %all-to-all-start.2) | async-done | bytes 1048608 | tf_op jit(solution)/shard_map/all_to_all | solution.py:42
  57.4 0.3 copy.157
  57.7 0.3 reshape.78
  58.0 0.0 copy-start.5
  58.0 2.6 fusion.46
  60.7 0.6 copy.108
  61.2 1.2 reshape.79
  62.5 3.5 %all-to-all-start.3 = ((bf16[8,4,32,512]{3,2,1,0:T(8,128)(2,1)}), bf16[8,4,32,512]{3,2,1,0:T(8,128)(2,1)S(1)}, u32[]{:S(2)}, u32[]{:S(2)}) async-start(bf16[8,4,32,512]{3,2,1,0:T(8,128)(2,1)} %reshape.79), calls=%async_computation.3 | async-start | bytes 2097152 | tf_op jit(solution)/shard_map/all_to_all | solution.py:70
  66.0 0.2 reduce-scatter.2.cloned.1.call-start
  66.2 1.5 collective-permute-done
  67.7 0.0 copy-done.5
  67.7 3.0 maximum_select_fusion.1
  70.8 2.5 collective-permute-start.1
  73.2 52.7 %all-to-all-done.3 = bf16[8,4,32,512]{3,2,1,0:T(8,128)(2,1)S(1)} async-done(((bf16[8,4,32,512]{3,2,1,0:T(8,128)(2,1)}), bf16[8,4,32,512]{3,2,1,0:T(8,128)(2,1)S(1)}, u32[]{:S(2)}, u32[]{:S(2)}) %all-to-all-start.3) | async-done | bytes 1048608 | tf_op jit(solution)/shard_map/all_to_all | solution.py:70
  126.0 0.1 copy.109
  126.1 0.0 all-gather.2.cloned.1.call-done
  126.1 7.6 %bitcast_convert_fusion = bf16[512,3072]{1,0:T(8,128)(2,1)} fusion(bf16[2,512,512]{2,1,0:T(8,128)(2,1)S(1)} %bitcast.85, bf16[2,512,3072]{2,1,0:T(8,128)(2,1)} %all-gather.2.cloned.1.call-done), kind=kOutput, calls=%fused_computation.9 | convolution fusion | flops 3222798336 | bytes 10485760 | tf_op jit(solution)/shard_map/fnh,fnd->hd/dot_general | solution.py:73
  133.7 0.0 reduce-scatter.2.cloned.1.call-update
  133.8 64.8 %collective-permute-done.1 = bf16[512,1536]{1,0:T(8,128)(2,1)} collective-permute-done((bf16[512,1536]{1,0:T(8,128)(2,1)}, bf16[512,1536]{1,0:T(8,128)(2,1)}, u32[]{:S(2)}, u32[]{:S(2)}) %collective-permute-start.1) | collective-permute-done | bytes 1572896 | tf_op jit(solution)/shard_map/ppermute | solution.py:64
  198.6 8.2 %fusion.42 = bf16[512,2,512]{0,2,1:T(8,128)(2,1)S(1)} fusion(bf16[2,512,3072]{2,1,0:T(8,128)(2,1)} %all-gather.2.cloned.1.call-done, bf16[512,1536]{1,0:T(8,128)(2,1)} %collective-permute-done.1, bf16[512,1536]{1,0:T(8,128)(2,1)} %maximum_select_fusion.1, pred[]{:T(512)S(6)} %eq.6), kind=kOutput, calls=%fused_computation.38 | convolution fusion | flops 3235905536 | bytes 10485761 | tf_op jit(solution)/shard_map/fnd,hd->fnh/dot_general | solution.py:74
  206.8 0.8 copy.85
  207.6 24.1 %all_to_all.60 = bf16[2,4,128,512]{3,1,0,2:T(4,128)(2,1)S(1)} all-to-all(bf16[2,4,128,512]{3,1,0,2:T(4,128)(2,1)S(1)} %copy.85), channel_id=1, replica_groups=mesh['parts'=2,'seq'=4,'sub'=4] {'seq'}, dimensions={2} | all-to-all | bytes 2097152 | tf_op jit(solution)/shard_map/all_to_all | solution.py:78
  231.6 0.3 copy.86
  231.9 0.1 copy.87
  232.0 0.3 reshape.68
  232.3 2.6 fusion.45
  234.9 0.6 copy.91
  235.5 0.4 reshape.71
  235.9 27.0 %all_to_all.61 = bf16[8,4,32,512]{3,2,1,0:T(8,128)(2,1)S(1)} all-to-all(bf16[8,4,32,512]{3,2,1,0:T(8,128)(2,1)S(1)} %reshape.71), channel_id=1, replica_groups=mesh['parts'=2,'seq'=4,'sub'=4] {'seq'}, dimensions={0} | all-to-all | bytes 2097152 | tf_op jit(solution)/shard_map/all_to_all | solution.py:88
  262.9 0.1 copy.158
  263.1 0.3 reshape.72
  263.4 0.7 copy.99
  264.0 5.9 %fusion.30 = bf16[2,4,128,512]{3,2,1,0:T(8,128)(2,1)} fusion(bf16[2,512,4,128]{1,3,2,0:T(8,128)(2,1)S(1)} %copy.99, f32[2,4,512,512]{2,3,1,0:T(8,128)} %get-tuple-element.23, f32[2,4,512]{2,1,0:T(4,128)S(1)} %get-tuple-element.22), kind=kOutput, calls=%fused_computation.32 | convolution fusion | flops 541589504 | bytes 10502144 | tf_op jit(solution)/shard_map/fhqk,fqhd->fkhd/dot_general | solution.py:97
  269.9 2.4 copy.113
  272.2 4.4 %fusion.51 = f32[2,4,512,512]{2,3,1,0:T(8,128)} fusion(bf16[2,512,4,128]{1,3,2,0:T(8,128)(2,1)S(1)} %copy.99, bf16[2,512,512]{2,1,0:T(8,128)(2,1)S(1)} %copy-done), kind=kOutput, calls=%fused_computation.43 | convolution fusion | flops 536870912 | bytes 10485760 | tf_op jit(solution)/shard_map/fqhd,fkhd->fhqk/dot_general | solution.py:103
  276.7 0.0 copy-done.4
  276.7 0.0 copy-start.2
  276.7 15.2 %fusion.36 = bf16[2,4,512,128]{2,3,1,0:T(8,128)(2,1)} fusion(bf16[2,512,4,128]{1,3,2,0:T(8,128)(2,1)S(1)} %bitcast.84, f32[2,4,512,512]{2,3,1,0:T(8,128)} %fusion.51, f32[2,4,512,512]{2,3,1,0:T(8,128)} %get-tuple-element.23, f32[2,4,512]{2,1,0:T(4,128)S(1)} %get-tuple-element.22), kind=kOutput, calls=%fused_computation.34 | convolution fusion | flops 552079872 | bytes 18890752 | tf_op jit(solution)/shard_map/fhqk,fkhd->fqhd/dot_general | solution.py:110
  291.9 2.3 copy.111
  294.2 0.0 copy-done.2
  294.2 12.3 %fusion.39 = bf16[2,4,512,128]{2,3,1,0:T(8,128)(2,1)S(1)} fusion(bf16[2,512,4,128]{1,3,2,0:T(8,128)(2,1)S(1)} %bitcast.82, f32[2,4,512,512]{2,3,1,0:T(8,128)} %fusion.51, f32[2,4,512,512]{2,3,1,0:T(8,128)} %get-tuple-element.23, f32[2,4,512]{2,1,0:T(4,128)S(1)} %get-tuple-element.22), kind=kOutput, calls=%fused_computation.35 | convolution fusion | flops 552079872 | bytes 18890752 | tf_op jit(solution)/shard_map/fhqk,fqhd->fkhd/dot_general | solution.py:113
  306.5 1.3 copy.112
  307.8 0.0 reduce-scatter.2.cloned.1.call-done
  307.8 2.4 convert_element_type.76
  (1 shorter events, 0.0 us)
Async XLA Ops:
  7.2 9.2 %copy-start = (bf16[2,512,512]{2,1,0:T(8,128)(2,1)S(1)}, bf16[2,512,512]{2,1,0:T(8,128)(2,1)}, u32[]{:S(2)}) copy-start(bf16[2,512,512]{2,1,0:T(8,128)(2,1)} %param.9) | copy-start | bytes 3145732
  7.2 118.9 %all-gather.2.cloned.1.call-start = ((), (), s32[]{:S(2)}) async-start(), calls=%async_computation.5 | async-start | bytes 7864320 | tf_op jit(solution)/shard_map/all_gather | solution.py:72
  9.4 7.0 %copy-start.1 = (bf16[2,512,512]{1,2,0:T(8,128)(2,1)}, bf16[2,512,512]{1,2,0:T(8,128)(2,1)S(1)}, u32[]{:S(2)}) copy-start(bf16[2,512,512]{1,2,0:T(8,128)(2,1)S(1)} %copy.121) | copy-start | bytes 3145732
  11.3 10.5 %copy-start.3 = (bf16[2,512,512]{1,2,0:T(8,128)(2,1)}, bf16[2,512,512]{1,2,0:T(8,128)(2,1)S(1)}, u32[]{:S(2)}) copy-start(bf16[2,512,512]{1,2,0:T(8,128)(2,1)S(1)} %copy.120) | copy-start | bytes 3145732
  24.9 32.5 %all-to-all-start.2 = ((bf16[2,4,128,512]{3,1,0,2:T(4,128)(2,1)}), bf16[2,4,128,512]{3,1,0,2:T(4,128)(2,1)S(1)}, u32[]{:S(2)}, u32[]{:S(2)}) async-start(bf16[2,4,128,512]{3,1,0,2:T(4,128)(2,1)} %copy.104), calls=%async_computation.2 | async-start | bytes 2097152 | tf_op jit(solution)/shard_map/all_to_all | solution.py:42
  31.6 36.1 %collective-permute-start = (bf16[512,768]{1,0:T(8,128)(2,1)}, bf16[512,768]{1,0:T(8,128)(2,1)}, u32[]{:S(2)}, u32[]{:S(2)}) collective-permute-start(bf16[512,768]{1,0:T(8,128)(2,1)} %param.12), channel_id=1, source_target_pairs={{0,4},{4,0},{8,12},{12,8},{1,5},{5,1},{9,13},{13,9},{2,6},{6,2},{1... | collective-permute-start | bytes 2359304 | tf_op jit(solution)/shard_map/ppermute | solution.py:64
  58.0 9.7 %copy-start.5 = (bf16[512,768]{1,0:T(8,128)(2,1)S(1)}, bf16[512,768]{1,0:T(8,128)(2,1)}, u32[]{:S(2)}) copy-start(bf16[512,768]{1,0:T(8,128)(2,1)} %param.12) | copy-start | bytes 2359300
  62.5 63.5 %all-to-all-start.3 = ((bf16[8,4,32,512]{3,2,1,0:T(8,128)(2,1)}), bf16[8,4,32,512]{3,2,1,0:T(8,128)(2,1)S(1)}, u32[]{:S(2)}, u32[]{:S(2)}) async-start(bf16[8,4,32,512]{3,2,1,0:T(8,128)(2,1)} %reshape.79), calls=%async_computation.3 | async-start | bytes 2097152 | tf_op jit(solution)/shard_map/all_to_all | solution.py:70
  66.0 241.8 %reduce-scatter.2.cloned.1.call-start = ((), (), s32[]{:S(2)}) async-start(), calls=%async_computation.6 | async-start | bytes 3932160 | tf_op jit(solution)/shard_map/reduce_scatter | solution.py:79
  70.8 127.8 %collective-permute-start.1 = (bf16[512,1536]{1,0:T(8,128)(2,1)}, bf16[512,1536]{1,0:T(8,128)(2,1)}, u32[]{:S(2)}, u32[]{:S(2)}) collective-permute-start(bf16[512,1536]{1,0:T(8,128)(2,1)} %maximum_select_fusion.1), channel_id=1, source_target_pairs={{0,8},{4,12},{8,0},{12,4},{1,9},{5,13},{9,1},{13,5},{2,10},{6,14},... | collective-permute-start | bytes 4718600 | tf_op jit(solution)/shard_map/ppermute | solution.py:64
  269.9 6.8 %copy-start.4 = (bf16[2,512,512]{1,2,0:T(8,128)(2,1)S(1)}, bf16[2,512,512]{1,2,0:T(8,128)(2,1)}, u32[]{:S(2)}) copy-start(bf16[2,512,512]{1,2,0:T(8,128)(2,1)} %copy-done.3) | copy-start | bytes 3145732
  276.7 17.5 %copy-start.2 = (bf16[2,512,512]{1,2,0:T(8,128)(2,1)S(1)}, bf16[2,512,512]{1,2,0:T(8,128)(2,1)}, u32[]{:S(2)}) copy-start(bf16[2,512,512]{1,2,0:T(8,128)(2,1)} %copy-done.1) | copy-start | bytes 3145732
Sparse Core Ops, SparseCore 0:
  9.6 49.0 all-gather.1
  133.9 77.7 reduce-scatter.1
